TPU v7x, 32 devices: a whole 2x2x4 slice. The times are simulated.
32 devices in a mesh: problem: 2 (over y), worker: 4 (over z), head: 4 (over x, core).
Axes of the slice: x: 2, y: 2, z: 4, core: 2. Of those that a mesh axis runs over, the one named last changes fastest.
Arguments:
- queries: bfloat16 [8, 4, 40, 128], P(('problem', 'worker'), None, 'head'), parts along dimension 0, may hold values from -60 to 60
- cache_keys: bfloat16 [8, 2048, 8, 128], P(('problem', 'worker'), None, 'head'), parts along dimension 0, may hold values from -6 to 6
- cache_values: bfloat16 [8, 2048, 8, 128], P(('problem', 'worker'), None, 'head'), parts along dimension 0, may hold values from -6 to 6
- new_keys: bfloat16 [8, 4, 8, 128], P(('problem', 'worker'), None, 'head'), parts along dimension 0, may hold values from -6 to 6
- new_values: bfloat16 [8, 4, 8, 128], P(('problem', 'worker'), None, 'head'), parts along dimension 0, may hold values from -6 to 6
- lengths: int32 [8, 4], P(('problem', 'worker')), parts along dimension 0, may hold values from 1 to 2048, as said below
Outputs:
- attended: bfloat16 [8, 4, 40, 128], P(('problem', 'worker'), None, 'head'), parts along dimension 0
There are 2 independent parts, one for each index of `problem`. A program takes and returns all parts, laid end to end along the dimension named above; each array names one. Nothing has to cross between parts.
Inputs may be any that keep to these rules, and one draw needn't show every extreme that they name: lengths never fall from one step to the next; some worker's length at the last step is exactly 2048.
All inputs are finite; a program needn't handle non-finite values.
Results may differ from a plain program's by a relative error of at most 0.005.
Values may be sent and summed in bfloat16 or wider, within the bound.
A program may use at most 64 MiB of HBM per device.

v0:
```python
import functools
import math

import jax
import jax.numpy as jnp
from jax import lax
from jax.experimental import pallas as pl
from jax.experimental.pallas import tpu as pltpu
from jax.sharding import PartitionSpec as P

masked_score = -1e30
lanes = 128
score_chunk = 512
value_chunk = 512
partial_type = jnp.bfloat16


def round_up(number, unit):
    return (number + unit - 1) // unit * unit


def partners_by_distance(own, workers):
    if workers > 8:
        return [lax.rem(own + step, workers) for step in range(1, workers)]
    table = [
        sorted((w for w in range(workers) if w != i), key=lambda w: (abs(w - i), w))
        for i in range(workers)
    ]
    partners = []
    for place in range(workers - 1):
        partner = jnp.int32(table[0][place])
        for i in range(1, workers):
            partner = jnp.where(own == i, table[i][place], partner)
        partners.append(partner)
    return partners


def kernel(
    workers,
    kv,
    steps,
    q_ref,
    k_ref,
    v_ref,
    nk_ref,
    nv_ref,
    len_ref,
    out_ref,
    q_in,
    q_pad,
    q_own,
    q_got,
    keys,
    values,
    new_keys,
    new_values,
    lens,
    score_buf,
    part_send,
    part_got,
    stat_send,
    stat_got,
    load_sem,
    q_send_sem,
    q_recv_sem,
    part_send_sem,
    part_recv_sem,
    stat_send_sem,
    stat_recv_sem,
):
    own = lax.axis_index("worker")
    rows_all, head_width = q_ref.shape
    per = rows_all // kv
    padded = q_pad.shape[0] // kv
    columns = k_ref.shape[0]
    fresh_columns = nk_ref.shape[0]
    factor = head_width ** (-0.5) * math.log2(math.e)
    partners = partners_by_distance(own, workers)

    barrier = pltpu.get_barrier_semaphore()
    for partner in partners:
        pl.semaphore_signal(
            barrier, inc=1, device_id={"worker": partner}, device_id_type=pl.DeviceIdType.MESH
        )

    loads = []
    for place, (source, target) in enumerate(
        (
            (q_ref, q_in),
            (len_ref, lens),
            (nk_ref, new_keys),
            (nv_ref, new_values),
            (k_ref, keys),
            (v_ref, values),
        )
    ):
        loads.append(pltpu.make_async_copy(source, target, load_sem.at[place]))
        loads[-1].start()

    loads[0].wait()
    q_pad[...] = jnp.zeros_like(q_pad)
    q_rows = q_in[...].astype(jnp.float32)
    for head in range(kv):
        q_pad[head * padded : head * padded + per, :] = q_rows[head * per : (head + 1) * per]
    q_own[...] = q_pad[...].astype(jnp.bfloat16)

    pl.semaphore_wait(barrier, workers - 1)
    sends = []

    def send(source, target, send_sem, recv_sem, partner):
        copy = pltpu.make_async_remote_copy(
            src_ref=source,
            dst_ref=target,
            send_sem=send_sem,
            recv_sem=recv_sem,
            device_id={"worker": partner},
            device_id_type=pl.DeviceIdType.MESH,
        )
        copy.start()
        sends.append(copy)

    for place, partner in reversed(list(enumerate(partners))):
        send(q_own, q_got.at[own], q_send_sem.at[place], q_recv_sem.at[own], partner)

    row_id = lax.broadcasted_iota(jnp.int32, (padded, lanes), 0)
    lane_id = lax.broadcasted_iota(jnp.int32, (padded, lanes), 1)
    row_step = lax.rem(row_id, steps)
    lane_head = lax.rem(lane_id, kv)
    loads[1].wait()
    limit = jnp.zeros((padded, lanes), jnp.int32)
    for step in range(steps):
        limit = jnp.where(row_step == step, lens[0, step], limit)
    limit = limit * kv - lane_id

    def fresh_limit(is_own):
        return jnp.minimum((row_step + (1 if is_own else 0)) * kv, fresh_columns) - lane_id

    loads[2].wait()
    loads[3].wait()
    tail = jnp.zeros((lanes - fresh_columns, head_width), jnp.float32)
    fresh_k = jnp.concatenate([new_keys[...].astype(jnp.float32), tail], axis=0)
    fresh_v = jnp.concatenate([new_values[...].astype(jnp.float32), tail], axis=0)
    fresh_k = fresh_k.astype(jnp.bfloat16)
    fresh_v = fresh_v.astype(jnp.bfloat16)

    full_row = lax.broadcasted_iota(jnp.int32, (kv * padded, lanes), 0)
    full_lane = lax.broadcasted_iota(jnp.int32, (kv * padded, lanes), 1)
    diagonal = full_row == full_lane

    def to_row(column):
        return jnp.sum(jnp.where(diagonal, column, 0.0), axis=0, keepdims=True)

    def to_column(row):
        return jnp.sum(jnp.where(diagonal, row, 0.0), axis=1, keepdims=True)

    def attend(queries, count, is_own, value_ready):
        best = [jnp.full((padded, lanes), masked_score, jnp.float32) for _ in range(count)]
        blocks = [
            (start, min(score_chunk, columns - start)) for start in range(0, columns, score_chunk)
        ] + [(columns, lanes)]
        for start, size in blocks:
            block = fresh_k if start == columns else keys[start : start + size, :]
            scores = lax.dot_general(
                queries, block, (((1,), (1,)), ((), ())), preferred_element_type=jnp.float32
            )
            for item in range(count):
                base = item * kv * padded
                for offset in range(0, size, lanes):
                    score = scores[base : base + padded, offset : offset + lanes]
                    for head in range(1, kv):
                        low = base + head * padded
                        score = jnp.where(
                            lane_head == head,
                            scores[low : low + padded, offset : offset + lanes],
                            score,
                        )
                    if start == columns:
                        seen = fresh_limit(is_own) > 0
                    else:
                        seen = limit > start + offset
                    score = jnp.where(seen, score, masked_score)
                    best[item] = jnp.maximum(best[item], score)
                    score_buf[
                        item * padded : (item + 1) * padded,
                        start + offset : start + offset + lanes,
                    ] = score
        maxima, pivots = [], []
        for item in range(count):
            heads = [
                jnp.max(
                    jnp.where(lane_head == head, best[item], masked_score), axis=1, keepdims=True
                )
                for head in range(kv)
            ]
            pivot = jnp.broadcast_to(heads[0], (padded, lanes))
            for head in range(1, kv):
                pivot = jnp.where(lane_head == head, heads[head], pivot)
            maxima.append(to_row(jnp.concatenate(heads, axis=0)))
            pivots.append(pivot)
        sums = [jnp.zeros((padded, lanes), jnp.float32) for _ in range(count)]
        outputs = jnp.zeros((count * kv * padded, head_width), jnp.float32)
        value_ready()
        blocks = [
            (start, min(value_chunk, columns - start)) for start in range(0, columns, value_chunk)
        ] + [(columns, lanes)]
        for start, size in blocks:
            pieces = []
            for offset in range(0, size, lanes):
                stack = []
                for item in range(count):
                    score = score_buf[
                        item * padded : (item + 1) * padded,
                        start + offset : start + offset + lanes,
                    ]
                    weight = jnp.exp2((score - pivots[item]) * factor)
                    sums[item] = sums[item] + weight
                    for head in range(kv):
                        stack.append(jnp.where(lane_head == head, weight, 0.0))
                pieces.append(jnp.concatenate(stack, axis=0).astype(jnp.bfloat16))
            weights = pieces[0] if len(pieces) == 1 else jnp.concatenate(pieces, axis=1)
            block = fresh_v if start == columns else values[start : start + size, :]
            outputs = outputs + jnp.dot(weights, block, preferred_element_type=jnp.float32)
        totals = []
        for item in range(count):
            heads = [
                jnp.sum(jnp.where(lane_head == head, sums[item], 0.0), axis=1, keepdims=True)
                for head in range(kv)
            ]
            totals.append(to_row(jnp.concatenate(heads, axis=0)))
        return maxima, totals, outputs

    loads[4].wait()
    own_max, own_total, own_out = attend(q_own[...], 1, True, loads[5].wait)
    own_max, own_total = own_max[0], own_total[0]

    def answer(place, partner):
        slot = q_got.at[partner]
        pltpu.make_async_copy(slot, slot, q_recv_sem.at[partner]).wait()
        maxima, totals, outputs = attend(q_got[partner], 1, False, lambda: None)
        stat_send[place, 0:1, :] = maxima[0]
        stat_send[place, 1:2, :] = totals[0]
        part_send[place] = outputs.astype(part_send.dtype)
        stat = pltpu.make_async_remote_copy(
            src_ref=stat_send.at[place],
            dst_ref=stat_got.at[own],
            send_sem=stat_send_sem.at[place],
            recv_sem=stat_recv_sem.at[own],
            device_id={"worker": partner},
            device_id_type=pl.DeviceIdType.MESH,
        )
        part = pltpu.make_async_remote_copy(
            src_ref=part_send.at[place],
            dst_ref=part_got.at[own],
            send_sem=part_send_sem.at[place],
            recv_sem=part_recv_sem.at[own],
            device_id={"worker": partner},
            device_id_type=pl.DeviceIdType.MESH,
        )
        stat.start()
        part.start()
        return stat, part

    if workers <= 8:
        for place, partner in enumerate(partners):
            sends.extend(answer(place, partner))
    else:

        def body(place, carry):
            answer(place, lax.rem(own + 1 + place, workers))
            return carry

        lax.fori_loop(0, workers - 1, body, 0)
        for place, partner in enumerate(partners):
            for source, sem in ((stat_send, stat_send_sem), (part_send, part_send_sem)):
                slot = source.at[place]
                pltpu.make_async_copy(slot, slot, sem.at[place]).wait()

    top = own_max
    for partner in partners:
        slot = stat_got.at[partner]
        pltpu.make_async_copy(slot, slot, stat_recv_sem.at[partner]).wait()
        top = jnp.maximum(top, stat_got[partner, 0:1, :])
    own_scale = jnp.exp2((own_max - top) * factor)
    total = own_total * own_scale
    scales = []
    for partner in partners:
        scale = jnp.exp2((stat_got[partner, 0:1, :] - top) * factor)
        total = total + stat_got[partner, 1:2, :] * scale
        scales.append(scale)
    merged = own_out * to_column(own_scale / total)
    columns_of = [to_column(scale / total) for scale in scales]
    for partner, column in zip(partners, columns_of):
        slot = part_got.at[partner]
        pltpu.make_async_copy(slot, slot, part_recv_sem.at[partner]).wait()
        merged = merged + part_got[partner].astype(jnp.float32) * column
    out_ref[...] = jnp.concatenate(
        [merged[head * padded : head * padded + per] for head in range(kv)], axis=0
    ).astype(out_ref.dtype)
    for copy in sends:
        copy.wait_send()


def local(queries, cache_keys, cache_values, new_keys, new_values, lengths):
    workers = lax.axis_size("worker")
    _, steps, q_local, head_width = queries.shape
    _, slots, kv, _ = cache_keys.shape
    rows = steps * q_local
    padded = round_up(rows // kv, 8)
    while kv * padded % 16:
        padded += 8
    full = kv * padded
    query_rows = queries.transpose(0, 2, 1, 3).reshape(rows, head_width)
    dma = pltpu.SemaphoreType.DMA
    bf16, f32 = jnp.bfloat16, jnp.float32
    out = pl.pallas_call(
        functools.partial(kernel, workers, kv, steps),
        out_shape=jax.ShapeDtypeStruct((rows, head_width), bf16),
        in_specs=[pl.BlockSpec(memory_space=pl.ANY)] * 6,
        out_specs=pl.BlockSpec(memory_space=pltpu.VMEM),
        scratch_shapes=[
            pltpu.VMEM((rows, head_width), bf16),
            pltpu.VMEM((full, head_width), f32),
            pltpu.VMEM((full, head_width), bf16),
            pltpu.VMEM((workers, full, head_width), bf16),
            pltpu.VMEM((slots * kv, head_width), bf16),
            pltpu.VMEM((slots * kv, head_width), bf16),
            pltpu.VMEM((steps * kv, head_width), bf16),
            pltpu.VMEM((steps * kv, head_width), bf16),
            pltpu.SMEM(lengths.shape, jnp.int32),
            pltpu.VMEM((padded, slots * kv + lanes), f32),
            pltpu.VMEM((workers, full, head_width), partial_type),
            pltpu.VMEM((workers, full, head_width), partial_type),
            pltpu.VMEM((workers, 2, lanes), f32),
            pltpu.VMEM((workers, 2, lanes), f32),
            dma((6,)),
            dma((workers,)),
            dma((workers,)),
            dma((workers,)),
            dma((workers,)),
            dma((workers,)),
            dma((workers,)),
        ],
        compiler_params=pltpu.CompilerParams(collective_id=0, has_side_effects=True),
    )(
        query_rows,
        cache_keys.reshape(slots * kv, head_width),
        cache_values.reshape(slots * kv, head_width),
        new_keys.reshape(steps * kv, head_width),
        new_values.reshape(steps * kv, head_width),
        lengths,
    )
    return out.reshape(1, q_local, steps, head_width).transpose(0, 2, 1, 3)


def solution(mesh):
    spread = P(("problem", "worker"), None, "head", None)
    return jax.shard_map(
        local,
        mesh=mesh,
        in_specs=(spread,) * 5 + (P(("problem", "worker"), None),),
        out_specs=spread,
        check_vma=False,
    )
```

profile of v0, /device:TPU:0, one launch (start us, length us, event | category | flops | bytes accessed | tf_op | source)
XLA Modules:
  0.0 15.5 jit_solution(12398307146601881801)
XLA Ops:
  0.0 14.2 %shard_map.64 = bf16[40,128]{1,0:T(8,128)(2,1)} custom-call(bf16[40,128]{1,0:T(8,128)(2,1)} %bitcast.13, bf16[4096,128]{1,0:T(8,128)(2,1)} %bitcast.10, bf16[4096,128]{1,0:T(8,128)(2,1)} %bitcast.11, bf16[8,128]{1,0:T(8,128)(2,1)} %bitcast.14, bf16[8,128]{1,0:T(8,128)(2,1)} %bitcast.15, s32[1,4]{1,0:T(1,128)} %len_ref.1), custom_call_target="tpu_custom_call" | custom-call | tf_op jit(solution)/shard_map/pallas_call | solution.py:315
  14.2 1.3 %copy.8 = bf16[1,4,10,128]{3,1,2,0:T(4,128)(2,1)} copy(bf16[1,4,10,128]{3,1,2,0:T(4,128)(2,1)} %bitcast.12) | data formatting | bytes 20480
where the time goes:
time: 15.8 us; the launch traced here: 15.5 us
  Pallas kernels  14.2 us (90%)
  local copies, waits for them, and re-layouts  1.31 us (8%)
    pallas_call x1, Pallas kernels, local(): pl.pallas_call(functools.partial(kernel, workers, kv, steps), out_shape=j...  14.2 us
    unnamed x1, local copies, waits for them, and re-layouts  1.31 us

commit v1 on v0

--- a/solution.py
+++ b/solution.py
@@ -314,7 +314,7 @@
     bf16, f32 = jnp.bfloat16, jnp.float32
     out = pl.pallas_call(
         functools.partial(kernel, workers, kv, steps),
-        out_shape=jax.ShapeDtypeStruct((rows, head_width), bf16),
+        out_shape=pltpu.VMEM((rows, head_width), bf16),
         in_specs=[pl.BlockSpec(memory_space=pl.ANY)] * 6,
         out_specs=pl.BlockSpec(memory_space=pltpu.VMEM),
         scratch_shapes=[

time: 15.8 us -> 14.4 us (0.911)
  local copies, waits for them, and re-layouts: 1.31 us -> 0.6 us
  Pallas kernels: 14.2 us -> 13.6 us
    unnamed x1, local copies, waits for them, and re-layouts: 1.31 us -> 0.6 us
    pallas_call x1, Pallas kernels: 14.2 us -> 13.6 us  [local(): pl.pallas_call(functools.partial(kernel, workers, kv, steps), out_shape=p...]
where the time goes in v1:
time: 14.4 us; the launch traced here: 14.2 us
  Pallas kernels  13.6 us (94%)
  local copies, waits for them, and re-layouts  0.6 us (4%)
    pallas_call x1, Pallas kernels, local(): pl.pallas_call(functools.partial(kernel, workers, kv, steps), out_shape=p...  13.6 us
    unnamed x1, local copies, waits for them, and re-layouts  0.6 us

profile of v1, /device:TPU:0, one launch (start us, length us, event | category | flops | bytes accessed | tf_op | source)
XLA Modules:
  0.0 14.2 jit_solution(4133375194543021906)
XLA Ops:
  0.0 13.6 %shard_map.64 = bf16[40,128]{1,0:T(8,128)(2,1)S(1)} custom-call(bf16[40,128]{1,0:T(8,128)(2,1)} %bitcast.13, bf16[4096,128]{1,0:T(8,128)(2,1)} %bitcast.11, bf16[4096,128]{1,0:T(8,128)(2,1)} %bitcast.12, bf16[8,128]{1,0:T(8,128)(2,1)} %bitcast.14, bf16[8,128]{1,0:T(8,128)(2,1)} %bitcast.15, s32[1,4]{1,0:T(1,128)} %len_ref.1), custom_call_target="tpu_custom_call" | custom-call | tf_op jit(solution)/shard_map/pallas_call | solution.py:315
  13.6 0.6 %copy.8 = bf16[1,4,10,128]{3,1,2,0:T(4,128)(2,1)} copy(bf16[1,4,10,128]{3,1,2,0:T(4,128)(2,1)S(1)} %bitcast.10) | data formatting | bytes 20480

commit v2 on v1

--- a/solution.py
+++ b/solution.py
@@ -78,7 +78,7 @@
     partners = partners_by_distance(own, workers)
 
     barrier = pltpu.get_barrier_semaphore()
-    for partner in partners:
+    for partner in reversed(partners):
         pl.semaphore_signal(
             barrier, inc=1, device_id={"worker": partner}, device_id_type=pl.DeviceIdType.MESH
         )
@@ -239,7 +239,6 @@
         maxima, totals, outputs = attend(q_got[partner], 1, False, lambda: None)
         stat_send[place, 0:1, :] = maxima[0]
         stat_send[place, 1:2, :] = totals[0]
-        part_send[place] = outputs.astype(part_send.dtype)
         stat = pltpu.make_async_remote_copy(
             src_ref=stat_send.at[place],
             dst_ref=stat_got.at[own],
@@ -257,12 +256,13 @@
             device_id_type=pl.DeviceIdType.MESH,
         )
         stat.start()
+        part_send[place] = outputs.astype(part_send.dtype)
         part.start()
         return stat, part
 
     if workers <= 8:
-        for place, partner in enumerate(partners):
-            sends.extend(answer(place, partner))
+        for place in [0] + list(range(workers - 2, 0, -1)):
+            sends.extend(answer(place, partners[place]))
     else:
 
         def body(place, carry):
@@ -275,24 +275,23 @@
                 slot = source.at[place]
                 pltpu.make_async_copy(slot, slot, sem.at[place]).wait()
 
-    top = own_max
-    for partner in partners:
+    top, total, merged = own_max, own_total, own_out
+    for place, partner in enumerate(partners):
         slot = stat_got.at[partner]
         pltpu.make_async_copy(slot, slot, stat_recv_sem.at[partner]).wait()
-        top = jnp.maximum(top, stat_got[partner, 0:1, :])
-    own_scale = jnp.exp2((own_max - top) * factor)
-    total = own_total * own_scale
-    scales = []
-    for partner in partners:
-        scale = jnp.exp2((stat_got[partner, 0:1, :] - top) * factor)
-        total = total + stat_got[partner, 1:2, :] * scale
-        scales.append(scale)
-    merged = own_out * to_column(own_scale / total)
-    columns_of = [to_column(scale / total) for scale in scales]
-    for partner, column in zip(partners, columns_of):
+        part_max, part_total = stat_got[partner, 0:1, :], stat_got[partner, 1:2, :]
+        joined = jnp.maximum(top, part_max)
+        kept = jnp.exp2((top - joined) * factor)
+        added = jnp.exp2((part_max - joined) * factor)
+        top, total = joined, total * kept + part_total * added
+        if place == workers - 2:
+            kept, added = kept / total, added / total
+        kept, added = to_column(kept), to_column(added)
         slot = part_got.at[partner]
         pltpu.make_async_copy(slot, slot, part_recv_sem.at[partner]).wait()
-        merged = merged + part_got[partner].astype(jnp.float32) * column
+        merged = merged * kept + part_got[partner].astype(jnp.float32) * added
+    if workers == 1:
+        merged = merged * to_column(1.0 / total)
     out_ref[...] = jnp.concatenate(
         [merged[head * padded : head * padded + per] for head in range(kv)], axis=0
     ).astype(out_ref.dtype)
@@ -314,7 +313,7 @@
     bf16, f32 = jnp.bfloat16, jnp.float32
     out = pl.pallas_call(
         functools.partial(kernel, workers, kv, steps),
-        out_shape=pltpu.VMEM((rows, head_width), bf16),
+        out_shape=pltpu.VMEM((rows, head_width), f32),
         in_specs=[pl.BlockSpec(memory_space=pl.ANY)] * 6,
         out_specs=pl.BlockSpec(memory_space=pltpu.VMEM),
         scratch_shapes=[
@@ -349,6 +348,7 @@
         new_values.reshape(steps * kv, head_width),
         lengths,
     )
+    out = out.astype(bf16)
     return out.reshape(1, q_local, steps, head_width).transpose(0, 2, 1, 3)
 
 

time: 14.4 us -> 14.2 us (0.986)
  other arithmetic: 0 us -> 0.6 us
  local copies, waits for them, and re-layouts: 0.6 us -> 0 us
  Pallas kernels: 13.6 us -> 13.4 us
    convert_element_type x0 -> x1, other arithmetic: none -> 0.6 us  [local(): out = out.astype(bf16)]
    unnamed x1 -> x0, local copies, waits for them, and re-layouts: 0.6 us -> none
    pallas_call x1, Pallas kernels: 13.6 us -> 13.4 us  [local(): pl.pallas_call(functools.partial(kernel, workers, kv, steps), out_shape=p...]
where the time goes in v2:
time: 14.2 us; the launch traced here: 14 us
  Pallas kernels  13.4 us (94%)
  other arithmetic  0.6 us (4%)
    pallas_call x1, Pallas kernels, local(): pl.pallas_call(functools.partial(kernel, workers, kv, steps), out_shape=p...  13.4 us
    convert_element_type x1, other arithmetic, local(): out = out.astype(bf16)  0.6 us

profile of v2, /device:TPU:0, one launch (start us, length us, event | category | flops | bytes accessed | tf_op | source)
XLA Modules:
  0.0 14.0 jit_solution(14062364370305861950)
XLA Ops:
  0.0 13.4 %shard_map.64 = f32[40,128]{1,0:T(8,128)S(1)} custom-call(bf16[40,128]{1,0:T(8,128)(2,1)} %bitcast.12, bf16[4096,128]{1,0:T(8,128)(2,1)} %bitcast.10, bf16[4096,128]{1,0:T(8,128)(2,1)} %bitcast.11, bf16[8,128]{1,0:T(8,128)(2,1)} %bitcast.13, bf16[8,128]{1,0:T(8,128)(2,1)} %bitcast.14, s32[1,4]{1,0:T(1,128)} %len_ref.1), custom_call_target="tpu_custom_call" | custom-call | tf_op jit(solution)/shard_map/pallas_call | solution.py:314
  13.4 0.6 %convert_element_type.3 = bf16[40,128]{1,0:T(8,128)(2,1)} convert(f32[40,128]{1,0:T(8,128)S(1)} %shard_map.64) | non-fusion elementwise | flops 5120 | bytes 30720 | tf_op jit(solution)/shard_map/convert_element_type | solution.py:351
